TPU v7x, 256 devices: a whole 4x4x8 slice. The times are simulated.
256 devices in a mesh: doc: 4 (over x), ctx: 16 (over z, core), head: 4 (over y).
Axes of the slice: x: 4, y: 4, z: 8, core: 2. Of those that a mesh axis runs over, the one named last changes fastest.
Arguments:
- queries: bfloat16 [1024, 16384], P(('doc', 'ctx'), 'head'), as said below
- doc_of: int32 [1024, 1], P(('doc', 'ctx')), may hold values from 0 to 3; in each aligned block of 16 rows (0 to 15, 16 to 31, ...) at most 6 rows name the same one
- doc_lengths: int32 [4], replicated, may hold values from 4096 to 16384, as said below
- rotated_key_levels: bfloat16 [4, 16384, 1024], P('doc', 'ctx', 'head'), may hold values from -8 to 7
- rotated_value_levels: bfloat16 [4, 16384, 1024], P('doc', 'ctx', 'head'), may hold values from -8 to 7
- key_level_scale: bfloat16 [4, 8, 16384], P('doc', 'head', 'ctx'), may hold values from 0.19921875 to 0.796875
- value_level_scale: bfloat16 [4, 8, 16384], P('doc', 'head', 'ctx'), may hold values from 0.099609375 to 0.3984375
Outputs:
- attended: bfloat16 [1024, 16384], P(('doc', 'ctx'))
Inputs may be any that keep to these rules, and one draw needn't show every extreme that they name: `queries`: query rows. `doc_of`: in the rows of one device no document is named by more than 6 requests, a bound that some block reaches. `doc_lengths`: some document is valid over all its positions.
All inputs are finite; a program needn't handle non-finite values.
Results may differ from a plain program's by a relative error of at most 0.02.
Values may be sent and summed in bfloat16 or wider, within the bound.
A program may use at most 128 MiB of HBM per device.

v0:
```python
import math

import jax
import jax.numpy as jnp
from jax import lax
from jax.sharding import PartitionSpec as P

HEAD_WIDTH = 128


def shifted(value, axis, steps):
    count = lax.axis_size(axis)
    pairs = [(source, (source + steps) % count) for source in range(count)]
    return lax.ppermute(value, axis, pairs)


def joined_along(blocks, dim):
    blocks = jnp.moveaxis(blocks, 0, dim)
    dims = blocks.shape
    return blocks.reshape(*dims[:dim], dims[dim] * dims[dim + 1], *dims[dim + 2 :])


def copy_for_each(array, axis):
    copies = jnp.broadcast_to(array, (lax.axis_size(axis), *array.shape))
    return lax.all_to_all(copies, axis, split_axis=0, concat_axis=0, tiled=True)


def gather_directly(array, axis, dim):
    return joined_along(copy_for_each(array, axis), dim)


def hadamard_signs():
    idx = jnp.arange(HEAD_WIDTH, dtype=jnp.int32)
    both = jnp.bitwise_and(idx[:, None], idx[None, :])
    parity = jnp.zeros_like(both)
    for bit in range(HEAD_WIDTH.bit_length()):
        parity = parity + jnp.bitwise_and(jnp.right_shift(both, bit), 1)
    return (1 - 2 * (parity % 2)).astype(jnp.float32)


def update_state(
    softmax_state,
    query_rows,
    key_block,
    value_block,
    key_block_scale,
    value_block_scale,
    valid_mask,
):
    inverse_total = 1.0 / math.sqrt(HEAD_WIDTH)
    current_maximum, current_denominator, current_weighted_sum = softmax_state
    score_block = jnp.einsum(
        "bkgd,skd->bkgs", query_rows, key_block, preferred_element_type=jnp.float32
    )
    score_block = (
        score_block * (key_block_scale.astype(jnp.float32) * inverse_total)[None, :, None, :]
    )
    score_block = jnp.where(valid_mask[None, None, None, :], score_block, jnp.float32(-1e30))
    new_max = jnp.maximum(current_maximum, jnp.max(score_block, axis=-1))
    probs = jnp.where(
        valid_mask[None, None, None, :], jnp.exp(score_block - new_max[..., None]), jnp.float32(0.0)
    )
    factor = jnp.exp(current_maximum - new_max)
    new_total = current_denominator * factor + jnp.sum(probs, axis=-1)
    weights = (probs * value_block_scale.astype(jnp.float32)[None, :, None, :]).astype(jnp.bfloat16)
    new_sum = current_weighted_sum * factor[..., None] + jnp.einsum(
        "bkgs,skd->bkgd", weights, value_block, preferred_element_type=jnp.float32
    )
    return (new_max, new_total, new_sum)


def absorb_block(
    softmax_state,
    query_rows,
    key_block,
    value_block,
    key_block_scale,
    value_block_scale,
    valid_mask,
):
    return update_state(
        softmax_state,
        query_rows,
        key_block,
        value_block,
        key_block_scale,
        value_block_scale,
        valid_mask,
    )


def shards(
    queries,
    doc_of,
    doc_lengths,
    rotated_key_levels,
    rotated_value_levels,
    key_level_scale,
    value_level_scale,
):
    inverse_total = 1.0 / math.sqrt(HEAD_WIDTH)
    signs = hadamard_signs()
    rows_home, width = queries.shape
    heads_dev = width // HEAD_WIDTH
    kv_dev = key_level_scale.shape[1]
    head_group = heads_dev // kv_dev
    shard_len = rotated_key_levels.shape[1]
    n_doc = lax.axis_size("doc")
    n_ctx = lax.axis_size("ctx")
    cap = max(2, 3 * rows_home // (2 * n_doc))
    rotated_rows = jnp.einsum(
        "rhd,de->rhe",
        queries.reshape(rows_home, heads_dev, HEAD_WIDTH),
        signs.astype(jnp.bfloat16),
        preferred_element_type=jnp.float32,
    )
    rotated_rows = (rotated_rows * inverse_total).astype(jnp.bfloat16).reshape(rows_home, width)
    target = doc_of[:, 0]
    onehot = (target[:, None] == jnp.arange(n_doc, dtype=jnp.int32)[None, :]).astype(jnp.int32)
    earlier = jnp.cumsum(onehot, axis=0) - onehot
    rank = jnp.sum(earlier * onehot, axis=1)
    slot = target * cap + rank
    placing = (jnp.arange(n_doc * cap, dtype=jnp.int32)[:, None] == slot[None, :]).astype(
        jnp.bfloat16
    )
    outgoing = (
        jnp.dot(placing, rotated_rows, preferred_element_type=jnp.float32)
        .astype(jnp.bfloat16)
        .reshape(n_doc, cap, width)
    )
    my_doc = lax.axis_index("doc")
    my_ctx = lax.axis_index("ctx")
    length = lax.dynamic_slice_in_dim(doc_lengths, my_doc, 1)[0]
    key_block = rotated_key_levels[0].reshape(shard_len, kv_dev, HEAD_WIDTH)
    value_block = rotated_value_levels[0].reshape(shard_len, kv_dev, HEAD_WIDTH)
    key_block_scale = key_level_scale[0]
    value_block_scale = value_level_scale[0]
    positions = jnp.arange(shard_len, dtype=jnp.int32)
    block = lax.all_to_all(outgoing, "doc", split_axis=0, concat_axis=0, tiled=True)
    count = block.shape[0] * block.shape[1]
    query_rows = block.reshape(count, kv_dev, head_group, HEAD_WIDTH)
    start_max = jnp.full((count, kv_dev, head_group), -1e30, jnp.float32)
    start_total = jnp.zeros((count, kv_dev, head_group), jnp.float32)
    start_sum = jnp.zeros((count, kv_dev, head_group, HEAD_WIDTH), jnp.float32)
    valid_mask = my_ctx * shard_len + positions < length

    def turn(step, carry):
        moving_parts, current_maximum, current_denominator, current_weighted_sum = carry
        current_maximum, current_denominator, current_weighted_sum = absorb_block(
            (current_maximum, current_denominator, current_weighted_sum),
            moving_parts,
            key_block,
            value_block,
            key_block_scale,
            value_block_scale,
            valid_mask,
        )
        moving_parts = shifted(moving_parts, "ctx", 1)
        current_maximum, current_denominator, current_weighted_sum = shifted(
            (current_maximum, current_denominator, current_weighted_sum), "ctx", 1
        )
        return (moving_parts, current_maximum, current_denominator, current_weighted_sum)

    _, current_maximum, current_denominator, current_weighted_sum = lax.fori_loop(
        0, n_ctx, turn, (query_rows, start_max, start_total, start_sum)
    )
    mixed = current_weighted_sum / current_denominator[..., None]
    result = (
        jnp.einsum("bkgd,de->bkge", mixed, signs, precision=lax.Precision.HIGHEST) * inverse_total
    )
    finished = result.astype(jnp.bfloat16).reshape(block.shape)
    returned = lax.all_to_all(finished, "doc", split_axis=0, concat_axis=0, tiled=True).reshape(
        n_doc * cap, width
    )
    mine = jnp.einsum("sr,sc->rc", placing, returned, preferred_element_type=jnp.float32).astype(
        jnp.bfloat16
    )
    return gather_directly(mine, "head", 1)


def solution(mesh):
    in_specs = (
        P(("doc", "ctx"), "head"),
        P(("doc", "ctx"), None),
        P(),
        P("doc", "ctx", "head"),
        P("doc", "ctx", "head"),
        P("doc", "head", "ctx"),
        P("doc", "head", "ctx"),
    )
    out_specs = P(("doc", "ctx"), None)
    return jax.shard_map(shards, mesh=mesh, in_specs=in_specs, out_specs=out_specs, check_vma=False)
```

profile of v0, /device:TPU:128, one launch (start us, length us, event | category | flops | bytes accessed | tf_op | source)
XLA Modules:
  0.0 271.4 jit_solution(14430468336746088423)
XLA Ops:
  2.3 0.9 copy.38
  4.5 4.3 %all-to-all-start = ((bf16[4,6,4096]{2,1,0:T(8,128)(2,1)}), bf16[4,6,4096]{2,1,0:T(8,128)(2,1)S(1)}, u32[]{:S(2)}, u32[]{:S(2)}) async-start(bf16[4,6,4096]{2,1,0:T(8,128)(2,1)} %reshape.42), calls=%async_computation | async-start | bytes 524288 | tf_op jit(solution)/shard_map/all_to_all | solution.py:139
  8.8 1.2 copy.27
  11.5 4.0 %all-to-all-done = bf16[4,6,4096]{2,1,0:T(8,128)(2,1)S(1)} async-done(((bf16[4,6,4096]{2,1,0:T(8,128)(2,1)}), bf16[4,6,4096]{2,1,0:T(8,128)(2,1)S(1)}, u32[]{:S(2)}, u32[]{:S(2)}) %all-to-all-start) | async-done | bytes 196640 | tf_op jit(solution)/shard_map/all_to_all | solution.py:139
  15.9 231.9 %while.17 = (s32[]{:T(128)}, bf16[24,2,16,128]{3,0,2,1:T(8,128)(2,1)S(1)}, f32[24,2,16]{0,2,1:T(8,128)S(1)}, f32[24,2,16]{0,2,1:T(8,128)S(1)}, f32[24,2,16,128]{...) while((s32[]{:T(128)}, ...), condition=%wide.region_5.6_spmd.clone, body=%wide.region_2.5_spmd.clone.sunk | while | flops 413869568 | bytes 14350621 | solution.py:164
  17.3 0.9 fusion.57
  18.3 1.3 fusion.58
  19.6 1.1 collective-permute-start
  20.7 1.1 collective-permute-start.2
  21.8 8.4 %collective-permute-done.1 = f32[24,2,16]{0,2,1:T(8,128)S(1)} collective-permute-done((f32[24,2,16]{0,2,1:T(8,128)S(1)}, f32[24,2,16]{0,2,1:T(8,128)S(1)}, u32[]{:S(2)}, u32[]{:S(2)}) %collective-permute-start.1) | collective-permute-done | bytes 3104 | tf_op jit(solution)/shard_map/while/body/eval_jaxpr/ppermute | solution.py:14
  31.8 0.9 fusion.57
  32.7 1.3 fusion.58
  34.1 1.0 collective-permute-start.2
  35.1 9.7 %collective-permute-done.1 = f32[24,2,16]{0,2,1:T(8,128)S(1)} collective-permute-done((f32[24,2,16]{0,2,1:T(8,128)S(1)}, f32[24,2,16]{0,2,1:T(8,128)S(1)}, u32[]{:S(2)}, u32[]{:S(2)}) %collective-permute-start.1) | collective-permute-done | bytes 3104 | tf_op jit(solution)/shard_map/while/body/eval_jaxpr/ppermute | solution.py:14
  47.2 1.3 fusion.58
  48.6 10.6 %collective-permute-done.1 = f32[24,2,16]{0,2,1:T(8,128)S(1)} collective-permute-done((f32[24,2,16]{0,2,1:T(8,128)S(1)}, f32[24,2,16]{0,2,1:T(8,128)S(1)}, u32[]{:S(2)}, u32[]{:S(2)}) %collective-permute-start.1) | collective-permute-done | bytes 3104 | tf_op jit(solution)/shard_map/while/body/eval_jaxpr/ppermute | solution.py:14
  60.8 0.9 fusion.57
  61.7 1.3 fusion.58
  63.1 10.6 %collective-permute-done.1 = f32[24,2,16]{0,2,1:T(8,128)S(1)} collective-permute-done((f32[24,2,16]{0,2,1:T(8,128)S(1)}, f32[24,2,16]{0,2,1:T(8,128)S(1)}, u32[]{:S(2)}, u32[]{:S(2)}) %collective-permute-start.1) | collective-permute-done | bytes 3104 | tf_op jit(solution)/shard_map/while/body/eval_jaxpr/ppermute | solution.py:14
  75.3 0.9 fusion.57
  76.2 1.3 fusion.58
  77.6 10.6 %collective-permute-done.1 = f32[24,2,16]{0,2,1:T(8,128)S(1)} collective-permute-done((f32[24,2,16]{0,2,1:T(8,128)S(1)}, f32[24,2,16]{0,2,1:T(8,128)S(1)}, u32[]{:S(2)}, u32[]{:S(2)}) %collective-permute-start.1) | collective-permute-done | bytes 3104 | tf_op jit(solution)/shard_map/while/body/eval_jaxpr/ppermute | solution.py:14
  89.8 0.9 fusion.57
  90.7 1.3 fusion.58
  92.1 10.6 %collective-permute-done.1 = f32[24,2,16]{0,2,1:T(8,128)S(1)} collective-permute-done((f32[24,2,16]{0,2,1:T(8,128)S(1)}, f32[24,2,16]{0,2,1:T(8,128)S(1)}, u32[]{:S(2)}, u32[]{:S(2)}) %collective-permute-start.1) | collective-permute-done | bytes 3104 | tf_op jit(solution)/shard_map/while/body/eval_jaxpr/ppermute | solution.py:14
  104.3 0.9 fusion.57
  105.2 1.3 fusion.58
  106.6 10.6 %collective-permute-done.1 = f32[24,2,16]{0,2,1:T(8,128)S(1)} collective-permute-done((f32[24,2,16]{0,2,1:T(8,128)S(1)}, f32[24,2,16]{0,2,1:T(8,128)S(1)}, u32[]{:S(2)}, u32[]{:S(2)}) %collective-permute-start.1) | collective-permute-done | bytes 3104 | tf_op jit(solution)/shard_map/while/body/eval_jaxpr/ppermute | solution.py:14
  119.7 1.3 fusion.58
  121.1 10.6 %collective-permute-done.1 = f32[24,2,16]{0,2,1:T(8,128)S(1)} collective-permute-done((f32[24,2,16]{0,2,1:T(8,128)S(1)}, f32[24,2,16]{0,2,1:T(8,128)S(1)}, u32[]{:S(2)}, u32[]{:S(2)}) %collective-permute-start.1) | collective-permute-done | bytes 3104 | tf_op jit(solution)/shard_map/while/body/eval_jaxpr/ppermute | solution.py:14
  134.2 1.3 fusion.58
  135.6 10.6 %collective-permute-done.1 = f32[24,2,16]{0,2,1:T(8,128)S(1)} collective-permute-done((f32[24,2,16]{0,2,1:T(8,128)S(1)}, f32[24,2,16]{0,2,1:T(8,128)S(1)}, u32[]{:S(2)}, u32[]{:S(2)}) %collective-permute-start.1) | collective-permute-done | bytes 3104 | tf_op jit(solution)/shard_map/while/body/eval_jaxpr/ppermute | solution.py:14
  148.7 1.3 fusion.58
  150.1 10.6 %collective-permute-done.1 = f32[24,2,16]{0,2,1:T(8,128)S(1)} collective-permute-done((f32[24,2,16]{0,2,1:T(8,128)S(1)}, f32[24,2,16]{0,2,1:T(8,128)S(1)}, u32[]{:S(2)}, u32[]{:S(2)}) %collective-permute-start.1) | collective-permute-done | bytes 3104 | tf_op jit(solution)/shard_map/while/body/eval_jaxpr/ppermute | solution.py:14
  163.2 1.3 fusion.58
  164.6 10.6 %collective-permute-done.1 = f32[24,2,16]{0,2,1:T(8,128)S(1)} collective-permute-done((f32[24,2,16]{0,2,1:T(8,128)S(1)}, f32[24,2,16]{0,2,1:T(8,128)S(1)}, u32[]{:S(2)}, u32[]{:S(2)}) %collective-permute-start.1) | collective-permute-done | bytes 3104 | tf_op jit(solution)/shard_map/while/body/eval_jaxpr/ppermute | solution.py:14
  177.7 1.3 fusion.58
  179.1 10.6 %collective-permute-done.1 = f32[24,2,16]{0,2,1:T(8,128)S(1)} collective-permute-done((f32[24,2,16]{0,2,1:T(8,128)S(1)}, f32[24,2,16]{0,2,1:T(8,128)S(1)}, u32[]{:S(2)}, u32[]{:S(2)}) %collective-permute-start.1) | collective-permute-done | bytes 3104 | tf_op jit(solution)/shard_map/while/body/eval_jaxpr/ppermute | solution.py:14
  192.2 1.3 fusion.58
  193.6 10.6 %collective-permute-done.1 = f32[24,2,16]{0,2,1:T(8,128)S(1)} collective-permute-done((f32[24,2,16]{0,2,1:T(8,128)S(1)}, f32[24,2,16]{0,2,1:T(8,128)S(1)}, u32[]{:S(2)}, u32[]{:S(2)}) %collective-permute-start.1) | collective-permute-done | bytes 3104 | tf_op jit(solution)/shard_map/while/body/eval_jaxpr/ppermute | solution.py:14
  206.7 1.3 fusion.58
  208.1 10.6 %collective-permute-done.1 = f32[24,2,16]{0,2,1:T(8,128)S(1)} collective-permute-done((f32[24,2,16]{0,2,1:T(8,128)S(1)}, f32[24,2,16]{0,2,1:T(8,128)S(1)}, u32[]{:S(2)}, u32[]{:S(2)}) %collective-permute-start.1) | collective-permute-done | bytes 3104 | tf_op jit(solution)/shard_map/while/body/eval_jaxpr/ppermute | solution.py:14
  221.1 1.3 fusion.58
  222.5 10.6 %collective-permute-done.1 = f32[24,2,16]{0,2,1:T(8,128)S(1)} collective-permute-done((f32[24,2,16]{0,2,1:T(8,128)S(1)}, f32[24,2,16]{0,2,1:T(8,128)S(1)}, u32[]{:S(2)}, u32[]{:S(2)}) %collective-permute-start.1) | collective-permute-done | bytes 3104 | tf_op jit(solution)/shard_map/while/body/eval_jaxpr/ppermute | solution.py:14
  235.6 1.3 fusion.58
  237.0 10.6 %collective-permute-done.1 = f32[24,2,16]{0,2,1:T(8,128)S(1)} collective-permute-done((f32[24,2,16]{0,2,1:T(8,128)S(1)}, f32[24,2,16]{0,2,1:T(8,128)S(1)}, u32[]{:S(2)}, u32[]{:S(2)}) %collective-permute-start.1) | collective-permute-done | bytes 3104 | tf_op jit(solution)/shard_map/while/body/eval_jaxpr/ppermute | solution.py:14
  248.8 9.1 %all_to_all.15 = bf16[4,6,4096]{2,1,0:T(8,128)(2,1)S(1)} all-to-all(bf16[4,6,4096]{2,1,0:T(8,128)(2,1)S(1)} %reshape.44), channel_id=1, replica_groups=mesh['doc'=4,'ctx'=16,'head'=4] {'doc'}, dimensions={0} | all-to-all | bytes 393216 | tf_op jit(solution)/shard_map/all_to_all | solution.py:172
  258.2 12.3 %all_to_all.16 = bf16[4,16,4096]{2,1,0:T(8,128)(2,1)S(1)} all-to-all(bf16[4,16,4096]{2,1,0:T(8,128)(2,1)S(1)} %broadcast_in_dim.47), channel_id=1, replica_groups=mesh['doc'=4,'ctx'=16,'head'=4] {'head'}, dimensions={0} | all-to-all | bytes 1048576 | tf_op jit(solution)/shard_map/all_to_all | solution.py:25
  (262 shorter events, 42.5 us)
Async XLA Ops:
  4.5 11.0 %all-to-all-start = ((bf16[4,6,4096]{2,1,0:T(8,128)(2,1)}), bf16[4,6,4096]{2,1,0:T(8,128)(2,1)S(1)}, u32[]{:S(2)}, u32[]{:S(2)}) async-start(bf16[4,6,4096]{2,1,0:T(8,128)(2,1)} %reshape.42), calls=%async_computation | async-start | bytes 524288 | tf_op jit(solution)/shard_map/all_to_all | solution.py:139
  19.5 10.9 %collective-permute-start.3 = (f32[24,2,16,128]{3,0,2,1:T(8,128)S(1)}, f32[24,2,16,128]{3,0,2,1:T(8,128)S(1)}, u32[]{:S(2)}, u32[]{:S(2)}) collective-permute-start(f32[24,2,16,128]{3,0,2,1:T(8,128)S(1)} %fusion.58), channel_id=1, source_target_pairs={{0,4},{4,8},{8,12},{12,16},{16,20},{20,24},{24,28},{28,32},{32,36}... | collective-permute-start | bytes 1179656 | tf_op jit(solution)/shard_map/while/body/eval_jaxpr/ppermute | solution.py:14
  19.6 10.9 %collective-permute-start = (bf16[24,2,16,128]{3,0,2,1:T(8,128)(2,1)S(1)}, bf16[24,2,16,128]{3,0,2,1:T(8,128)(2,1)S(1)}, u32[]{:S(2)}, u32[]{:S(2)}) collective-permute-start(bf16[24,2,16,128]{3,0,2,1:T(8,128)(2,1)S(1)} %copy.52), channel_id=1, source_target_pairs={{0,4},{4,8},{8,12},{12,16},{16,20},{20,24},{24,28},{28,32},{32,36}... | collective-permute-start | bytes 589832 | tf_op jit(solution)/shard_map/while/body/eval_jaxpr/ppermute | solution.py:14
  34.0 10.9 %collective-permute-start.3 = (f32[24,2,16,128]{3,0,2,1:T(8,128)S(1)}, f32[24,2,16,128]{3,0,2,1:T(8,128)S(1)}, u32[]{:S(2)}, u32[]{:S(2)}) collective-permute-start(f32[24,2,16,128]{3,0,2,1:T(8,128)S(1)} %fusion.58), channel_id=1, source_target_pairs={{0,4},{4,8},{8,12},{12,16},{16,20},{20,24},{24,28},{28,32},{32,36}... | collective-permute-start | bytes 1179656 | tf_op jit(solution)/shard_map/while/body/eval_jaxpr/ppermute | solution.py:14
  34.1 10.9 %collective-permute-start = (bf16[24,2,16,128]{3,0,2,1:T(8,128)(2,1)S(1)}, bf16[24,2,16,128]{3,0,2,1:T(8,128)(2,1)S(1)}, u32[]{:S(2)}, u32[]{:S(2)}) collective-permute-start(bf16[24,2,16,128]{3,0,2,1:T(8,128)(2,1)S(1)} %copy.52), channel_id=1, source_target_pairs={{0,4},{4,8},{8,12},{12,16},{16,20},{20,24},{24,28},{28,32},{32,36}... | collective-permute-start | bytes 589832 | tf_op jit(solution)/shard_map/while/body/eval_jaxpr/ppermute | solution.py:14
  34.1 10.8 %collective-permute-start.2 = (f32[24,2,16]{0,2,1:T(8,128)S(1)}, f32[24,2,16]{0,2,1:T(8,128)S(1)}, u32[]{:S(2)}, u32[]{:S(2)}) collective-permute-start(f32[24,2,16]{0,2,1:T(8,128)S(1)} %get-tuple-element.218), channel_id=1, source_target_pairs={{0,4},{4,8},{8,12},{12,16},{16,20},{20,24},{24,28},{28,32},{32,36}... | collective-permute-start | bytes 9224 | tf_op jit(solution)/shard_map/while/body/eval_jaxpr/ppermute | solution.py:14
  48.5 10.9 %collective-permute-start.3 = (f32[24,2,16,128]{3,0,2,1:T(8,128)S(1)}, f32[24,2,16,128]{3,0,2,1:T(8,128)S(1)}, u32[]{:S(2)}, u32[]{:S(2)}) collective-permute-start(f32[24,2,16,128]{3,0,2,1:T(8,128)S(1)} %fusion.58), channel_id=1, source_target_pairs={{0,4},{4,8},{8,12},{12,16},{16,20},{20,24},{24,28},{28,32},{32,36}... | collective-permute-start | bytes 1179656 | tf_op jit(solution)/shard_map/while/body/eval_jaxpr/ppermute | solution.py:14
  48.5 10.9 %collective-permute-start = (bf16[24,2,16,128]{3,0,2,1:T(8,128)(2,1)S(1)}, bf16[24,2,16,128]{3,0,2,1:T(8,128)(2,1)S(1)}, u32[]{:S(2)}, u32[]{:S(2)}) collective-permute-start(bf16[24,2,16,128]{3,0,2,1:T(8,128)(2,1)S(1)} %copy.52), channel_id=1, source_target_pairs={{0,4},{4,8},{8,12},{12,16},{16,20},{20,24},{24,28},{28,32},{32,36}... | collective-permute-start | bytes 589832 | tf_op jit(solution)/shard_map/while/body/eval_jaxpr/ppermute | solution.py:14
  48.6 10.8 %collective-permute-start.2 = (f32[24,2,16]{0,2,1:T(8,128)S(1)}, f32[24,2,16]{0,2,1:T(8,128)S(1)}, u32[]{:S(2)}, u32[]{:S(2)}) collective-permute-start(f32[24,2,16]{0,2,1:T(8,128)S(1)} %get-tuple-element.218), channel_id=1, source_target_pairs={{0,4},{4,8},{8,12},{12,16},{16,20},{20,24},{24,28},{28,32},{32,36}... | collective-permute-start | bytes 9224 | tf_op jit(solution)/shard_map/while/body/eval_jaxpr/ppermute | solution.py:14
  63.0 10.9 %collective-permute-start.3 = (f32[24,2,16,128]{3,0,2,1:T(8,128)S(1)}, f32[24,2,16,128]{3,0,2,1:T(8,128)S(1)}, u32[]{:S(2)}, u32[]{:S(2)}) collective-permute-start(f32[24,2,16,128]{3,0,2,1:T(8,128)S(1)} %fusion.58), channel_id=1, source_target_pairs={{0,4},{4,8},{8,12},{12,16},{16,20},{20,24},{24,28},{28,32},{32,36}... | collective-permute-start | bytes 1179656 | tf_op jit(solution)/shard_map/while/body/eval_jaxpr/ppermute | solution.py:14
  63.0 10.9 %collective-permute-start = (bf16[24,2,16,128]{3,0,2,1:T(8,128)(2,1)S(1)}, bf16[24,2,16,128]{3,0,2,1:T(8,128)(2,1)S(1)}, u32[]{:S(2)}, u32[]{:S(2)}) collective-permute-start(bf16[24,2,16,128]{3,0,2,1:T(8,128)(2,1)S(1)} %copy.52), channel_id=1, source_target_pairs={{0,4},{4,8},{8,12},{12,16},{16,20},{20,24},{24,28},{28,32},{32,36}... | collective-permute-start | bytes 589832 | tf_op jit(solution)/shard_map/while/body/eval_jaxpr/ppermute | solution.py:14
  63.1 10.8 %collective-permute-start.2 = (f32[24,2,16]{0,2,1:T(8,128)S(1)}, f32[24,2,16]{0,2,1:T(8,128)S(1)}, u32[]{:S(2)}, u32[]{:S(2)}) collective-permute-start(f32[24,2,16]{0,2,1:T(8,128)S(1)} %get-tuple-element.218), channel_id=1, source_target_pairs={{0,4},{4,8},{8,12},{12,16},{16,20},{20,24},{24,28},{28,32},{32,36}... | collective-permute-start | bytes 9224 | tf_op jit(solution)/shard_map/while/body/eval_jaxpr/ppermute | solution.py:14
  77.5 10.9 %collective-permute-start.3 = (f32[24,2,16,128]{3,0,2,1:T(8,128)S(1)}, f32[24,2,16,128]{3,0,2,1:T(8,128)S(1)}, u32[]{:S(2)}, u32[]{:S(2)}) collective-permute-start(f32[24,2,16,128]{3,0,2,1:T(8,128)S(1)} %fusion.58), channel_id=1, source_target_pairs={{0,4},{4,8},{8,12},{12,16},{16,20},{20,24},{24,28},{28,32},{32,36}... | collective-permute-start | bytes 1179656 | tf_op jit(solution)/shard_map/while/body/eval_jaxpr/ppermute | solution.py:14
  77.5 10.9 %collective-permute-start = (bf16[24,2,16,128]{3,0,2,1:T(8,128)(2,1)S(1)}, bf16[24,2,16,128]{3,0,2,1:T(8,128)(2,1)S(1)}, u32[]{:S(2)}, u32[]{:S(2)}) collective-permute-start(bf16[24,2,16,128]{3,0,2,1:T(8,128)(2,1)S(1)} %copy.52), channel_id=1, source_target_pairs={{0,4},{4,8},{8,12},{12,16},{16,20},{20,24},{24,28},{28,32},{32,36}... | collective-permute-start | bytes 589832 | tf_op jit(solution)/shard_map/while/body/eval_jaxpr/ppermute | solution.py:14
  77.6 10.8 %collective-permute-start.2 = (f32[24,2,16]{0,2,1:T(8,128)S(1)}, f32[24,2,16]{0,2,1:T(8,128)S(1)}, u32[]{:S(2)}, u32[]{:S(2)}) collective-permute-start(f32[24,2,16]{0,2,1:T(8,128)S(1)} %get-tuple-element.218), channel_id=1, source_target_pairs={{0,4},{4,8},{8,12},{12,16},{16,20},{20,24},{24,28},{28,32},{32,36}... | collective-permute-start | bytes 9224 | tf_op jit(solution)/shard_map/while/body/eval_jaxpr/ppermute | solution.py:14
  92.0 10.9 %collective-permute-start.3 = (f32[24,2,16,128]{3,0,2,1:T(8,128)S(1)}, f32[24,2,16,128]{3,0,2,1:T(8,128)S(1)}, u32[]{:S(2)}, u32[]{:S(2)}) collective-permute-start(f32[24,2,16,128]{3,0,2,1:T(8,128)S(1)} %fusion.58), channel_id=1, source_target_pairs={{0,4},{4,8},{8,12},{12,16},{16,20},{20,24},{24,28},{28,32},{32,36}... | collective-permute-start | bytes 1179656 | tf_op jit(solution)/shard_map/while/body/eval_jaxpr/ppermute | solution.py:14
  92.0 10.9 %collective-permute-start = (bf16[24,2,16,128]{3,0,2,1:T(8,128)(2,1)S(1)}, bf16[24,2,16,128]{3,0,2,1:T(8,128)(2,1)S(1)}, u32[]{:S(2)}, u32[]{:S(2)}) collective-permute-start(bf16[24,2,16,128]{3,0,2,1:T(8,128)(2,1)S(1)} %copy.52), channel_id=1, source_target_pairs={{0,4},{4,8},{8,12},{12,16},{16,20},{20,24},{24,28},{28,32},{32,36}... | collective-permute-start | bytes 589832 | tf_op jit(solution)/shard_map/while/body/eval_jaxpr/ppermute | solution.py:14
  92.1 10.8 %collective-permute-start.2 = (f32[24,2,16]{0,2,1:T(8,128)S(1)}, f32[24,2,16]{0,2,1:T(8,128)S(1)}, u32[]{:S(2)}, u32[]{:S(2)}) collective-permute-start(f32[24,2,16]{0,2,1:T(8,128)S(1)} %get-tuple-element.218), channel_id=1, source_target_pairs={{0,4},{4,8},{8,12},{12,16},{16,20},{20,24},{24,28},{28,32},{32,36}... | collective-permute-start | bytes 9224 | tf_op jit(solution)/shard_map/while/body/eval_jaxpr/ppermute | solution.py:14
  106.5 10.9 %collective-permute-start.3 = (f32[24,2,16,128]{3,0,2,1:T(8,128)S(1)}, f32[24,2,16,128]{3,0,2,1:T(8,128)S(1)}, u32[]{:S(2)}, u32[]{:S(2)}) collective-permute-start(f32[24,2,16,128]{3,0,2,1:T(8,128)S(1)} %fusion.58), channel_id=1, source_target_pairs={{0,4},{4,8},{8,12},{12,16},{16,20},{20,24},{24,28},{28,32},{32,36}... | collective-permute-start | bytes 1179656 | tf_op jit(solution)/shard_map/while/body/eval_jaxpr/ppermute | solution.py:14
  106.5 10.9 %collective-permute-start = (bf16[24,2,16,128]{3,0,2,1:T(8,128)(2,1)S(1)}, bf16[24,2,16,128]{3,0,2,1:T(8,128)(2,1)S(1)}, u32[]{:S(2)}, u32[]{:S(2)}) collective-permute-start(bf16[24,2,16,128]{3,0,2,1:T(8,128)(2,1)S(1)} %copy.52), channel_id=1, source_target_pairs={{0,4},{4,8},{8,12},{12,16},{16,20},{20,24},{24,28},{28,32},{32,36}... | collective-permute-start | bytes 589832 | tf_op jit(solution)/shard_map/while/body/eval_jaxpr/ppermute | solution.py:14
  106.6 10.8 %collective-permute-start.2 = (f32[24,2,16]{0,2,1:T(8,128)S(1)}, f32[24,2,16]{0,2,1:T(8,128)S(1)}, u32[]{:S(2)}, u32[]{:S(2)}) collective-permute-start(f32[24,2,16]{0,2,1:T(8,128)S(1)} %get-tuple-element.218), channel_id=1, source_target_pairs={{0,4},{4,8},{8,12},{12,16},{16,20},{20,24},{24,28},{28,32},{32,36}... | collective-permute-start | bytes 9224 | tf_op jit(solution)/shard_map/while/body/eval_jaxpr/ppermute | solution.py:14
  121.0 10.9 %collective-permute-start.3 = (f32[24,2,16,128]{3,0,2,1:T(8,128)S(1)}, f32[24,2,16,128]{3,0,2,1:T(8,128)S(1)}, u32[]{:S(2)}, u32[]{:S(2)}) collective-permute-start(f32[24,2,16,128]{3,0,2,1:T(8,128)S(1)} %fusion.58), channel_id=1, source_target_pairs={{0,4},{4,8},{8,12},{12,16},{16,20},{20,24},{24,28},{28,32},{32,36}... | collective-permute-start | bytes 1179656 | tf_op jit(solution)/shard_map/while/body/eval_jaxpr/ppermute | solution.py:14
  121.0 10.9 %collective-permute-start = (bf16[24,2,16,128]{3,0,2,1:T(8,128)(2,1)S(1)}, bf16[24,2,16,128]{3,0,2,1:T(8,128)(2,1)S(1)}, u32[]{:S(2)}, u32[]{:S(2)}) collective-permute-start(bf16[24,2,16,128]{3,0,2,1:T(8,128)(2,1)S(1)} %copy.52), channel_id=1, source_target_pairs={{0,4},{4,8},{8,12},{12,16},{16,20},{20,24},{24,28},{28,32},{32,36}... | collective-permute-start | bytes 589832 | tf_op jit(solution)/shard_map/while/body/eval_jaxpr/ppermute | solution.py:14
  121.1 10.8 %collective-permute-start.2 = (f32[24,2,16]{0,2,1:T(8,128)S(1)}, f32[24,2,16]{0,2,1:T(8,128)S(1)}, u32[]{:S(2)}, u32[]{:S(2)}) collective-permute-start(f32[24,2,16]{0,2,1:T(8,128)S(1)} %get-tuple-element.218), channel_id=1, source_target_pairs={{0,4},{4,8},{8,12},{12,16},{16,20},{20,24},{24,28},{28,32},{32,36}... | collective-permute-start | bytes 9224 | tf_op jit(solution)/shard_map/while/body/eval_jaxpr/ppermute | solution.py:14
  135.5 10.9 %collective-permute-start.3 = (f32[24,2,16,128]{3,0,2,1:T(8,128)S(1)}, f32[24,2,16,128]{3,0,2,1:T(8,128)S(1)}, u32[]{:S(2)}, u32[]{:S(2)}) collective-permute-start(f32[24,2,16,128]{3,0,2,1:T(8,128)S(1)} %fusion.58), channel_id=1, source_target_pairs={{0,4},{4,8},{8,12},{12,16},{16,20},{20,24},{24,28},{28,32},{32,36}... | collective-permute-start | bytes 1179656 | tf_op jit(solution)/shard_map/while/body/eval_jaxpr/ppermute | solution.py:14
  135.5 10.9 %collective-permute-start = (bf16[24,2,16,128]{3,0,2,1:T(8,128)(2,1)S(1)}, bf16[24,2,16,128]{3,0,2,1:T(8,128)(2,1)S(1)}, u32[]{:S(2)}, u32[]{:S(2)}) collective-permute-start(bf16[24,2,16,128]{3,0,2,1:T(8,128)(2,1)S(1)} %copy.52), channel_id=1, source_target_pairs={{0,4},{4,8},{8,12},{12,16},{16,20},{20,24},{24,28},{28,32},{32,36}... | collective-permute-start | bytes 589832 | tf_op jit(solution)/shard_map/while/body/eval_jaxpr/ppermute | solution.py:14
  135.6 10.8 %collective-permute-start.2 = (f32[24,2,16]{0,2,1:T(8,128)S(1)}, f32[24,2,16]{0,2,1:T(8,128)S(1)}, u32[]{:S(2)}, u32[]{:S(2)}) collective-permute-start(f32[24,2,16]{0,2,1:T(8,128)S(1)} %get-tuple-element.218), channel_id=1, source_target_pairs={{0,4},{4,8},{8,12},{12,16},{16,20},{20,24},{24,28},{28,32},{32,36}... | collective-permute-start | bytes 9224 | tf_op jit(solution)/shard_map/while/body/eval_jaxpr/ppermute | solution.py:14
  150.0 10.9 %collective-permute-start.3 = (f32[24,2,16,128]{3,0,2,1:T(8,128)S(1)}, f32[24,2,16,128]{3,0,2,1:T(8,128)S(1)}, u32[]{:S(2)}, u32[]{:S(2)}) collective-permute-start(f32[24,2,16,128]{3,0,2,1:T(8,128)S(1)} %fusion.58), channel_id=1, source_target_pairs={{0,4},{4,8},{8,12},{12,16},{16,20},{20,24},{24,28},{28,32},{32,36}... | collective-permute-start | bytes 1179656 | tf_op jit(solution)/shard_map/while/body/eval_jaxpr/ppermute | solution.py:14
  150.0 10.9 %collective-permute-start = (bf16[24,2,16,128]{3,0,2,1:T(8,128)(2,1)S(1)}, bf16[24,2,16,128]{3,0,2,1:T(8,128)(2,1)S(1)}, u32[]{:S(2)}, u32[]{:S(2)}) collective-permute-start(bf16[24,2,16,128]{3,0,2,1:T(8,128)(2,1)S(1)} %copy.52), channel_id=1, source_target_pairs={{0,4},{4,8},{8,12},{12,16},{16,20},{20,24},{24,28},{28,32},{32,36}... | collective-permute-start | bytes 589832 | tf_op jit(solution)/shard_map/while/body/eval_jaxpr/ppermute | solution.py:14
  150.0 10.8 %collective-permute-start.2 = (f32[24,2,16]{0,2,1:T(8,128)S(1)}, f32[24,2,16]{0,2,1:T(8,128)S(1)}, u32[]{:S(2)}, u32[]{:S(2)}) collective-permute-start(f32[24,2,16]{0,2,1:T(8,128)S(1)} %get-tuple-element.218), channel_id=1, source_target_pairs={{0,4},{4,8},{8,12},{12,16},{16,20},{20,24},{24,28},{28,32},{32,36}... | collective-permute-start | bytes 9224 | tf_op jit(solution)/shard_map/while/body/eval_jaxpr/ppermute | solution.py:14
  164.5 10.9 %collective-permute-start.3 = (f32[24,2,16,128]{3,0,2,1:T(8,128)S(1)}, f32[24,2,16,128]{3,0,2,1:T(8,128)S(1)}, u32[]{:S(2)}, u32[]{:S(2)}) collective-permute-start(f32[24,2,16,128]{3,0,2,1:T(8,128)S(1)} %fusion.58), channel_id=1, source_target_pairs={{0,4},{4,8},{8,12},{12,16},{16,20},{20,24},{24,28},{28,32},{32,36}... | collective-permute-start | bytes 1179656 | tf_op jit(solution)/shard_map/while/body/eval_jaxpr/ppermute | solution.py:14
  164.5 10.9 %collective-permute-start = (bf16[24,2,16,128]{3,0,2,1:T(8,128)(2,1)S(1)}, bf16[24,2,16,128]{3,0,2,1:T(8,128)(2,1)S(1)}, u32[]{:S(2)}, u32[]{:S(2)}) collective-permute-start(bf16[24,2,16,128]{3,0,2,1:T(8,128)(2,1)S(1)} %copy.52), channel_id=1, source_target_pairs={{0,4},{4,8},{8,12},{12,16},{16,20},{20,24},{24,28},{28,32},{32,36}... | collective-permute-start | bytes 589832 | tf_op jit(solution)/shard_map/while/body/eval_jaxpr/ppermute | solution.py:14
  164.5 10.8 %collective-permute-start.2 = (f32[24,2,16]{0,2,1:T(8,128)S(1)}, f32[24,2,16]{0,2,1:T(8,128)S(1)}, u32[]{:S(2)}, u32[]{:S(2)}) collective-permute-start(f32[24,2,16]{0,2,1:T(8,128)S(1)} %get-tuple-element.218), channel_id=1, source_target_pairs={{0,4},{4,8},{8,12},{12,16},{16,20},{20,24},{24,28},{28,32},{32,36}... | collective-permute-start | bytes 9224 | tf_op jit(solution)/shard_map/while/body/eval_jaxpr/ppermute | solution.py:14
  179.0 10.9 %collective-permute-start.3 = (f32[24,2,16,128]{3,0,2,1:T(8,128)S(1)}, f32[24,2,16,128]{3,0,2,1:T(8,128)S(1)}, u32[]{:S(2)}, u32[]{:S(2)}) collective-permute-start(f32[24,2,16,128]{3,0,2,1:T(8,128)S(1)} %fusion.58), channel_id=1, source_target_pairs={{0,4},{4,8},{8,12},{12,16},{16,20},{20,24},{24,28},{28,32},{32,36}... | collective-permute-start | bytes 1179656 | tf_op jit(solution)/shard_map/while/body/eval_jaxpr/ppermute | solution.py:14
  179.0 10.9 %collective-permute-start = (bf16[24,2,16,128]{3,0,2,1:T(8,128)(2,1)S(1)}, bf16[24,2,16,128]{3,0,2,1:T(8,128)(2,1)S(1)}, u32[]{:S(2)}, u32[]{:S(2)}) collective-permute-start(bf16[24,2,16,128]{3,0,2,1:T(8,128)(2,1)S(1)} %copy.52), channel_id=1, source_target_pairs={{0,4},{4,8},{8,12},{12,16},{16,20},{20,24},{24,28},{28,32},{32,36}... | collective-permute-start | bytes 589832 | tf_op jit(solution)/shard_map/while/body/eval_jaxpr/ppermute | solution.py:14
  179.0 10.8 %collective-permute-start.2 = (f32[24,2,16]{0,2,1:T(8,128)S(1)}, f32[24,2,16]{0,2,1:T(8,128)S(1)}, u32[]{:S(2)}, u32[]{:S(2)}) collective-permute-start(f32[24,2,16]{0,2,1:T(8,128)S(1)} %get-tuple-element.218), channel_id=1, source_target_pairs={{0,4},{4,8},{8,12},{12,16},{16,20},{20,24},{24,28},{28,32},{32,36}... | collective-permute-start | bytes 9224 | tf_op jit(solution)/shard_map/while/body/eval_jaxpr/ppermute | solution.py:14
  193.4 10.9 %collective-permute-start.3 = (f32[24,2,16,128]{3,0,2,1:T(8,128)S(1)}, f32[24,2,16,128]{3,0,2,1:T(8,128)S(1)}, u32[]{:S(2)}, u32[]{:S(2)}) collective-permute-start(f32[24,2,16,128]{3,0,2,1:T(8,128)S(1)} %fusion.58), channel_id=1, source_target_pairs={{0,4},{4,8},{8,12},{12,16},{16,20},{20,24},{24,28},{28,32},{32,36}... | collective-permute-start | bytes 1179656 | tf_op jit(solution)/shard_map/while/body/eval_jaxpr/ppermute | solution.py:14
  193.5 10.9 %collective-permute-start = (bf16[24,2,16,128]{3,0,2,1:T(8,128)(2,1)S(1)}, bf16[24,2,16,128]{3,0,2,1:T(8,128)(2,1)S(1)}, u32[]{:S(2)}, u32[]{:S(2)}) collective-permute-start(bf16[24,2,16,128]{3,0,2,1:T(8,128)(2,1)S(1)} %copy.52), channel_id=1, source_target_pairs={{0,4},{4,8},{8,12},{12,16},{16,20},{20,24},{24,28},{28,32},{32,36}... | collective-permute-start | bytes 589832 | tf_op jit(solution)/shard_map/while/body/eval_jaxpr/ppermute | solution.py:14
  193.5 10.8 %collective-permute-start.2 = (f32[24,2,16]{0,2,1:T(8,128)S(1)}, f32[24,2,16]{0,2,1:T(8,128)S(1)}, u32[]{:S(2)}, u32[]{:S(2)}) collective-permute-start(f32[24,2,16]{0,2,1:T(8,128)S(1)} %get-tuple-element.218), channel_id=1, source_target_pairs={{0,4},{4,8},{8,12},{12,16},{16,20},{20,24},{24,28},{28,32},{32,36}... | collective-permute-start | bytes 9224 | tf_op jit(solution)/shard_map/while/body/eval_jaxpr/ppermute | solution.py:14
  207.9 10.9 %collective-permute-start.3 = (f32[24,2,16,128]{3,0,2,1:T(8,128)S(1)}, f32[24,2,16,128]{3,0,2,1:T(8,128)S(1)}, u32[]{:S(2)}, u32[]{:S(2)}) collective-permute-start(f32[24,2,16,128]{3,0,2,1:T(8,128)S(1)} %fusion.58), channel_id=1, source_target_pairs={{0,4},{4,8},{8,12},{12,16},{16,20},{20,24},{24,28},{28,32},{32,36}... | collective-permute-start | bytes 1179656 | tf_op jit(solution)/shard_map/while/body/eval_jaxpr/ppermute | solution.py:14
  208.0 10.9 %collective-permute-start = (bf16[24,2,16,128]{3,0,2,1:T(8,128)(2,1)S(1)}, bf16[24,2,16,128]{3,0,2,1:T(8,128)(2,1)S(1)}, u32[]{:S(2)}, u32[]{:S(2)}) collective-permute-start(bf16[24,2,16,128]{3,0,2,1:T(8,128)(2,1)S(1)} %copy.52), channel_id=1, source_target_pairs={{0,4},{4,8},{8,12},{12,16},{16,20},{20,24},{24,28},{28,32},{32,36}... | collective-permute-start | bytes 589832 | tf_op jit(solution)/shard_map/while/body/eval_jaxpr/ppermute | solution.py:14
  208.0 10.8 %collective-permute-start.2 = (f32[24,2,16]{0,2,1:T(8,128)S(1)}, f32[24,2,16]{0,2,1:T(8,128)S(1)}, u32[]{:S(2)}, u32[]{:S(2)}) collective-permute-start(f32[24,2,16]{0,2,1:T(8,128)S(1)} %get-tuple-element.218), channel_id=1, source_target_pairs={{0,4},{4,8},{8,12},{12,16},{16,20},{20,24},{24,28},{28,32},{32,36}... | collective-permute-start | bytes 9224 | tf_op jit(solution)/shard_map/while/body/eval_jaxpr/ppermute | solution.py:14
  222.4 10.9 %collective-permute-start.3 = (f32[24,2,16,128]{3,0,2,1:T(8,128)S(1)}, f32[24,2,16,128]{3,0,2,1:T(8,128)S(1)}, u32[]{:S(2)}, u32[]{:S(2)}) collective-permute-start(f32[24,2,16,128]{3,0,2,1:T(8,128)S(1)} %fusion.58), channel_id=1, source_target_pairs={{0,4},{4,8},{8,12},{12,16},{16,20},{20,24},{24,28},{28,32},{32,36}... | collective-permute-start | bytes 1179656 | tf_op jit(solution)/shard_map/while/body/eval_jaxpr/ppermute | solution.py:14
  222.5 10.9 %collective-permute-start = (bf16[24,2,16,128]{3,0,2,1:T(8,128)(2,1)S(1)}, bf16[24,2,16,128]{3,0,2,1:T(8,128)(2,1)S(1)}, u32[]{:S(2)}, u32[]{:S(2)}) collective-permute-start(bf16[24,2,16,128]{3,0,2,1:T(8,128)(2,1)S(1)} %copy.52), channel_id=1, source_target_pairs={{0,4},{4,8},{8,12},{12,16},{16,20},{20,24},{24,28},{28,32},{32,36}... | collective-permute-start | bytes 589832 | tf_op jit(solution)/shard_map/while/body/eval_jaxpr/ppermute | solution.py:14
  222.5 10.8 %collective-permute-start.2 = (f32[24,2,16]{0,2,1:T(8,128)S(1)}, f32[24,2,16]{0,2,1:T(8,128)S(1)}, u32[]{:S(2)}, u32[]{:S(2)}) collective-permute-start(f32[24,2,16]{0,2,1:T(8,128)S(1)} %get-tuple-element.218), channel_id=1, source_target_pairs={{0,4},{4,8},{8,12},{12,16},{16,20},{20,24},{24,28},{28,32},{32,36}... | collective-permute-start | bytes 9224 | tf_op jit(solution)/shard_map/while/body/eval_jaxpr/ppermute | solution.py:14
  236.9 10.9 %collective-permute-start.3 = (f32[24,2,16,128]{3,0,2,1:T(8,128)S(1)}, f32[24,2,16,128]{3,0,2,1:T(8,128)S(1)}, u32[]{:S(2)}, u32[]{:S(2)}) collective-permute-start(f32[24,2,16,128]{3,0,2,1:T(8,128)S(1)} %fusion.58), channel_id=1, source_target_pairs={{0,4},{4,8},{8,12},{12,16},{16,20},{20,24},{24,28},{28,32},{32,36}... | collective-permute-start | bytes 1179656 | tf_op jit(solution)/shard_map/while/body/eval_jaxpr/ppermute | solution.py:14
  237.0 10.9 %collective-permute-start = (bf16[24,2,16,128]{3,0,2,1:T(8,128)(2,1)S(1)}, bf16[24,2,16,128]{3,0,2,1:T(8,128)(2,1)S(1)}, u32[]{:S(2)}, u32[]{:S(2)}) collective-permute-start(bf16[24,2,16,128]{3,0,2,1:T(8,128)(2,1)S(1)} %copy.52), channel_id=1, source_target_pairs={{0,4},{4,8},{8,12},{12,16},{16,20},{20,24},{24,28},{28,32},{32,36}... | collective-permute-start | bytes 589832 | tf_op jit(solution)/shard_map/while/body/eval_jaxpr/ppermute | solution.py:14
  237.0 10.8 %collective-permute-start.2 = (f32[24,2,16]{0,2,1:T(8,128)S(1)}, f32[24,2,16]{0,2,1:T(8,128)S(1)}, u32[]{:S(2)}, u32[]{:S(2)}) collective-permute-start(f32[24,2,16]{0,2,1:T(8,128)S(1)} %get-tuple-element.218), channel_id=1, source_target_pairs={{0,4},{4,8},{8,12},{12,16},{16,20},{20,24},{24,28},{28,32},{32,36}... | collective-permute-start | bytes 9224 | tf_op jit(solution)/shard_map/while/body/eval_jaxpr/ppermute | solution.py:14
  (21 other events, 221.4 us)
where the time goes:
time: 272 us; the launch traced here: 271 us
  waiting for transfers between devices  173 us (64%)
  matrix products  32.8 us (12%)
  other arithmetic  27.4 us (10%)
  blocking collectives  21.4 us (8%)
  starting transfers between devices  8.62 us (3%)
  local copies, waits for them, and re-layouts  6.25 us (2%)
    ppermute x64, waiting for transfers between devices, shifted(): return lax.ppermute(value, axis, pairs)  169 us
    dot_general x16, matrix products, update_state(): jnp.einsum('bkgs,skd->bkgd', weights, value_block, preferred_element_type...  20.5 us
    reduce_sum x16, other arithmetic, update_state(): new_total = current_denominator * factor + jnp.sum(probs, axis=-1)  14.3 us
    all_to_all x1, blocking collectives, copy_for_each(): return lax.all_to_all(copies, axis, split_axis=0, concat_axis=0, tiled=True)  12.3 us
    dot_general x16, matrix products, update_state(): jnp.einsum('bkgd,skd->bkgs', query_rows, key_block, preferred_element_typ...  11.1 us
    lt x16, other arithmetic, shards(): valid_mask = my_ctx * shard_len + positions < length  10.2 us
    all_to_all x1, blocking collectives, shards(): lax.all_to_all(finished, 'doc', split_axis=0, concat_axis=0, tiled=True)  9.07 us
  transfers between devices with their start and end apart: 65, of which 33 were waited for; matrix products, arithmetic and copies ran while one was open for 1% of the time, Pallas kernels for 0%

commit v1 on v0

v1 whole, which is shorter than its diff:
```python
import functools
import math

import jax
import jax.numpy as jnp
import numpy as np
from jax import lax
from jax.experimental import pallas as pl
from jax.experimental.pallas import tpu as pltpu
from jax.sharding import PartitionSpec as P

HEAD_WIDTH = 128
GROUP = 16
SUBS = 2
MESH = pl.DeviceIdType.MESH
C = 1.0 / math.sqrt(HEAD_WIDTH)
LOG2E = math.log2(math.e)
F32 = jnp.float32
BF16 = jnp.bfloat16


def hadamard():
    i = np.arange(HEAD_WIDTH)
    both = i[:, None] & i[None, :]
    parity = np.zeros_like(both)
    for bit in range(7):
        parity ^= (both >> bit) & 1
    return (1 - 2 * parity).astype(np.float32)


def kernel(
    NX,
    NZ,
    NY,
    CAP,
    q_ref,
    doc_ref,
    len_ref,
    h_ref,
    ks_ref,
    vs_ref,
    k_ref,
    v_ref,
    out_ref,
    flat,
    rq,
    sendq,
    qbuf,
    kraw,
    vraw,
    ksb,
    vsb,
    kaug,
    vaug,
    sbuf,
    pacc,
    pmax,
    ptot,
    sacc,
    sml,
    racc,
    rml,
    fin,
    ret,
    obuf,
    loc_sem,
    kv_send,
    kv_recv,
    xq_send,
    xq_recv,
    ag_send,
    ag_recv,
    rs_send,
    rs_recv,
    rm_send,
    rm_recv,
    ret_send,
    ret_recv,
    y_send,
    y_recv,
):
    ix = lax.axis_index("doc")
    ic = lax.axis_index("ctx")
    iy = lax.axis_index("head")
    z, k = ic // 2, ic % 2
    L = NZ // 2
    rows = q_ref.shape[0]
    heads = q_ref.shape[1] // HEAD_WIDTH
    half_n = NX * CAP
    span = k_ref.shape[0]
    zp, zm = lax.rem(z + 1, NZ), lax.rem(z + NZ - 1, NZ)

    def dev(x, c, y):
        return (x, c, y)

    up, down = dev(ix, 2 * zp + k, iy), dev(ix, 2 * zm + k, iy)
    partner = dev(ix, 2 * z + (1 - k), iy)
    peers = [partner, up, down]
    for a in range(1, NX):
        for c in range(2):
            peers.append(dev(lax.rem(ix + a, NX), 2 * z + c, iy))
    for b in range(1, NY):
        peers.append(dev(ix, ic, lax.rem(iy + b, NY)))

    def remote(src, dst, ssem, rsem, device):
        return pltpu.make_async_remote_copy(
            src_ref=src,
            dst_ref=dst,
            send_sem=ssem,
            recv_sem=rsem,
            device_id=device,
            device_id_type=MESH,
        )

    own = pl.ds(pl.multiple_of(k * HEAD_WIDTH, HEAD_WIDTH), HEAD_WIDTH)
    other = pl.ds(pl.multiple_of((1 - k) * HEAD_WIDTH, HEAD_WIDTH), HEAD_WIDTH)
    local = [
        pltpu.make_async_copy(k_ref.at[:, own], kraw.at[k], loc_sem.at[0]),
        pltpu.make_async_copy(v_ref.at[:, own], vraw.at[k], loc_sem.at[1]),
        pltpu.make_async_copy(ks_ref, ksb.at[k], loc_sem.at[2]),
        pltpu.make_async_copy(vs_ref, vsb.at[k], loc_sem.at[3]),
    ]
    for copy in local:
        copy.start()

    barrier = pltpu.get_barrier_semaphore()
    for peer in peers:
        pl.semaphore_signal(barrier, inc=1, device_id=peer, device_id_type=MESH)

    for h in range(heads):
        flat[pl.ds(h, rows, stride=heads), :] = q_ref[
            :, h * HEAD_WIDTH : (h + 1) * HEAD_WIDTH
        ].astype(F32)
    signs = h_ref[...]
    rotated = jnp.dot(flat[...].astype(BF16), signs, preferred_element_type=F32) * F32(C)
    rq[...] = rotated.astype(BF16).reshape(rows, heads, HEAD_WIDTH)

    docs = [doc_ref[r, 0] for r in range(rows)]
    slots = []
    for r in range(rows):
        rank = jnp.int32(0)
        for e in range(r):
            rank = rank + jnp.where(docs[e] == docs[r], 1, 0)
        slots.append(docs[r] * CAP + rank)
    for d in range(NX):
        for s in range(CAP):
            at = jnp.int32(0)
            for r in range(1, rows):
                at = at + jnp.where(slots[r] == d * CAP + s, r, 0)
            request = rq[at]
            for g in range(2):
                sendq[d, g, s] = request[g * GROUP : (g + 1) * GROUP]

    pl.semaphore_wait(barrier, len(peers))

    mine = pl.ds(k * half_n + ix * CAP, CAP)
    xq = []
    for a in range(NX):
        for c in range(2):
            g = lax.rem(k + c, 2)
            xd = lax.rem(ix + a, NX)
            if a == 0 and c == 0:
                self_copy = pltpu.make_async_copy(
                    sendq.at[xd, g], qbuf.at[0, mine], loc_sem.at[4]
                )
                self_copy.start()
                continue
            copy = remote(
                sendq.at[xd, g],
                qbuf.at[0, mine],
                xq_send.at[a, c],
                xq_recv.at[a, c],
                dev(xd, 2 * z + g, iy),
            )
            copy.start()
            xq.append(copy)

    kv = [
        remote(k_ref.at[:, other], kraw.at[k], kv_send.at[0], kv_recv.at[0], partner),
        remote(v_ref.at[:, other], vraw.at[k], kv_send.at[1], kv_recv.at[1], partner),
        remote(ks_ref, ksb.at[k], kv_send.at[2], kv_recv.at[2], partner),
        remote(vs_ref, vsb.at[k], kv_send.at[3], kv_recv.at[3], partner),
    ]
    for copy in kv:
        copy.start()

    self_copy.wait()
    for copy in xq:
        copy.wait_recv()

    sub_n = half_n // SUBS

    def piece(h, u):
        return pl.ds(h * half_n + u * sub_n, sub_n)

    def forward(h, u, o_from, o_to, sem, device):
        return remote(
            qbuf.at[o_from, piece(h, u)],
            qbuf.at[o_to, piece(h, u)],
            ag_send.at[h, u, sem],
            ag_recv.at[h, u, o_to],
            device,
        )

    way = ((up, down), (down, up))
    for u in range(SUBS):
        for h in range(2):
            forward(h, u, 0, 1, 0, way[h][0]).start()
            if NZ - 1 > L:
                forward(h, u, 0, NZ - 1, NZ, way[h][1]).start()

    for copy in local:
        copy.wait()
    for copy in kv:
        copy.wait_recv()

    length = len_ref[ix]
    base = z * (2 * span)
    first = None
    for c in range(2):
        krow = jnp.where(k == 0, ksb[c].astype(F32)[0:1], ksb[c].astype(F32)[1:2])
        vrow = jnp.where(k == 0, vsb[c].astype(F32)[0:1], vsb[c].astype(F32)[1:2])
        krow = krow * F32(C * LOG2E)
        for j in range(span // 128):
            part = slice(j * 128, (j + 1) * 128)
            dest = slice(c * span + j * 128, c * span + (j + 1) * 128)
            start = base + c * span + j * 128
            scale = jnp.broadcast_to(krow[:, part], (128, 128)).T
            keys = kraw[c, part, :].astype(F32) * scale
            if first is None:
                first = keys[0:1]
            at = start + lax.broadcasted_iota(jnp.int32, (128, 128), 0)
            keys = jnp.where(at < length, keys, first)
            high = keys.astype(BF16)
            kaug[dest, 0:128] = high
            kaug[dest, 128:256] = (keys - high.astype(F32)).astype(BF16)
            at = start + lax.broadcasted_iota(jnp.int32, (128, 128), 1)
            values = vraw[c, part, :].astype(F32).T * vrow[:, part]
            vaug[0:128, dest] = jnp.where(at < length, values, 0.0).astype(BF16)
            vaug[128:144, dest] = jnp.where(at[0:16] < length, 1.0, 0.0).astype(BF16)

    tiles = 2 * half_n * GROUP // 256
    chunk = 256
    chunks = 2 * span // chunk

    def attend(o, tile):
        q = qbuf[o, pl.ds(tile * 16, 16)].reshape(256, HEAD_WIDTH)
        qq = jnp.concatenate([q, q], axis=1)
        top = None
        for i in range(chunks):
            part = slice(i * chunk, (i + 1) * chunk)
            s = lax.dot_general(
                kaug[part, :], qq, (((1,), (1,)), ((), ())), preferred_element_type=F32
            )
            sbuf[part, :] = s
            t = jnp.max(s.reshape(chunk // 8, 8, 256), axis=0)
            top = t if top is None else jnp.maximum(top, t)
        top = jnp.max(top, axis=0, keepdims=True)
        acc = None
        for i in range(chunks):
            part = slice(i * chunk, (i + 1) * chunk)
            p = jnp.exp2(sbuf[part, :] - top).astype(BF16)
            a = jnp.dot(vaug[:, part], p, preferred_element_type=F32)
            acc = a if acc is None else acc + a
        top = jnp.where(jnp.full((1, 256), base, jnp.int32) < length, top, F32(-1e30))
        for i in range(2):
            lanes = slice(i * 128, (i + 1) * 128)
            pacc[o, tile * 2 + i] = acc[0:128, lanes]
            ptot[o, tile * 2 + i] = acc[128:129, lanes]
            pmax[o, tile * 2 + i] = top[:, lanes]

    def attend_slot(o):
        @pl.loop(0, tiles)
        def _(tile):
            attend(o, tile)

    def gather_step(s, u):
        for h in range(2):
            forward(h, u, s, s, s, partner).wait_recv()

            @pl.when(s < L)
            def _():
                forward(h, u, s, s + 1, s, way[h][0]).start()

            @pl.when(s < NZ - L)
            def _():
                forward(h, u, NZ - s, NZ - s, 0, partner).wait_recv()

            @pl.when(s < NZ - L - 1)
            def _():
                forward(h, u, NZ - s, NZ - s - 1, NZ - s, way[h][1]).start()

    @pl.loop(1, L + 1)
    def _(s):
        count = jnp.where(s == 1, tiles, jnp.where(s == L, tiles, 2 * tiles))
        each = count // SUBS

        for u in range(SUBS):
            begin = u * each
            end = count if u == SUBS - 1 else (u + 1) * each

            def body(n, carry):
                o = jnp.where(n < tiles, jnp.where(s == 1, 0, NZ - s + 1), s - 1)
                attend(o, lax.rem(n, tiles))
                return carry

            lax.fori_loop(begin, end, body, 0)
            gather_step(s, u)

    groups = half_n * GROUP // 128

    def send_state(h, o_from, o_to, device):
        return (
            remote(
                sacc.at[h, o_from],
                racc.at[h, o_to],
                rs_send.at[h, o_from],
                rs_recv.at[h, o_to],
                device,
            ),
            remote(
                sml.at[h, o_from],
                rml.at[h, o_to],
                rm_send.at[h, o_from],
                rm_recv.at[h, o_to],
                device,
            ),
        )

    def wait_state(h, o):
        remote(sacc.at[h, 0], racc.at[h, o], rs_send.at[h, 0], rs_recv.at[h, o], partner).wait_recv()
        remote(sml.at[h, 0], rml.at[h, o], rm_send.at[h, 0], rm_recv.at[h, o], partner).wait_recv()

    def first_state(h, o, o_to, device):
        for g in range(groups):
            at = h * groups + g
            sacc[h, o, g] = pacc[o, at].astype(BF16)
            sml[h, o, g : g + 1] = pmax[o, at]
            sml[h, o, 4 + g : 5 + g] = ptot[o, at]
        for copy in send_state(h, o, o_to, device):
            copy.start()

    def merged(h, g, state, o_in):
        m1, l1, a1 = state
        m2 = rml[h, o_in, g : g + 1]
        l2 = rml[h, o_in, 4 + g : 5 + g]
        m = jnp.maximum(m1, m2)
        f1, f2 = jnp.exp2(m1 - m), jnp.exp2(m2 - m)
        return m, l1 * f1 + l2 * f2, a1 * f1 + racc[h, o_in, g].astype(F32) * f2

    def pass_on(h, o, o_to, device):
        wait_state(h, o)
        for g in range(groups):
            at = h * groups + g
            m, l, a = merged(h, g, (pmax[o, at], ptot[o, at], pacc[o, at]), o)
            sacc[h, o, g] = a.astype(BF16)
            sml[h, o, g : g + 1] = m
            sml[h, o, 4 + g : 5 + g] = l
        for copy in send_state(h, o, o_to, device):
            copy.start()

    if L + 1 < NZ:
        for h in range(2):
            first_state(h, L + 1, L + 2, way[h][0])
    attend_slot(L)
    for h in range(2):
        first_state(h, L, L - 1, way[h][1])
    if L > 1:
        attend_slot(L - 1)

    @pl.loop(0, L - 1)
    def _(n):
        s = L - 1 - n
        for h in range(2):
            pass_on(h, s, s - 1, way[h][1])

            @pl.when(s > 1)
            def _():
                o = NZ - s + 1
                pass_on(h, o, o + 1, way[h][0])

    for h in range(2):
        if NZ - 1 > L:
            wait_state(h, NZ)
        wait_state(h, 0)
        for g in range(groups):
            at = h * groups + g
            state = (pmax[0, at], ptot[0, at], pacc[0, at])
            if NZ - 1 > L:
                state = merged(h, g, state, NZ)
            _, l, a = merged(h, g, state, 0)
            x = a * (F32(C) / l)
            high = x.astype(BF16)
            low = (x - high.astype(F32)).astype(BF16)
            y = jnp.dot(signs, high, preferred_element_type=F32) + jnp.dot(
                signs, low, preferred_element_type=F32
            )
            fin[pl.ds(at * 8, 8)] = y.T.astype(BF16).reshape(8, GROUP, HEAD_WIDTH)

    returns = []
    for a in range(NX):
        for c in range(2):
            h = lax.rem(k + c, 2)
            xd = lax.rem(ix + a, NX)
            src = fin.at[pl.ds(h * half_n + xd * CAP, CAP)]
            dst = ret.at[pl.ds((ix * 2 + k) * CAP, CAP)]
            if a == 0 and c == 0:
                self_copy = pltpu.make_async_copy(src, dst, loc_sem.at[4])
                self_copy.start()
                continue
            copy = remote(
                src, dst, ret_send.at[a, c], ret_recv.at[a, c], dev(xd, 2 * z + h, iy)
            )
            copy.start()
            returns.append(copy)
    self_copy.wait()
    for copy in returns:
        copy.wait_recv()

    for r in range(rows):
        for g in range(2):
            at = (docs[r] * 2 + g) * CAP + (slots[r] - docs[r] * CAP)
            flat[r * heads + g * GROUP : r * heads + (g + 1) * GROUP, :] = ret[at].astype(F32)
    for h in range(heads):
        obuf[iy, :, h * HEAD_WIDTH : (h + 1) * HEAD_WIDTH] = flat[
            pl.ds(h, rows, stride=heads), :
        ].astype(BF16)

    width = q_ref.shape[1]

    def out_copy(y, sem):
        cols = pl.ds(pl.multiple_of(y * width, width), width)
        return pltpu.make_async_copy(obuf.at[y], out_ref.at[:, cols], loc_sem.at[5 + sem])

    outs = [out_copy(iy, 0)]
    outs[0].start()
    if NY > 1:
        yp, ym = lax.rem(iy + 1, NY), lax.rem(iy + NY - 1, NY)
        right, left = dev(ix, ic, yp), dev(ix, ic, ym)
        lanes = (slice(0, width // 2), slice(width // 2, width))

        def y_copy(y, part, sem, device):
            ref = obuf.at[y, :, lanes[part]]
            return remote(ref, ref, y_send.at[sem], y_recv.at[sem], device)

        sends = [
            y_copy(iy, 0, 0, right),
            y_copy(iy, 1, 1, left),
            y_copy(iy, 1, 2, right),
            y_copy(iy, 0, 3, left),
        ]
        for copy in sends:
            copy.start()
        y_copy(ym, 0, 0, right).wait_recv()
        relay = [y_copy(ym, 0, 4, right)]
        relay[0].start()
        y_copy(yp, 1, 1, left).wait_recv()
        relay.append(y_copy(yp, 1, 5, left))
        relay[1].start()
        y_copy(ym, 1, 2, right).wait_recv()
        outs.append(out_copy(ym, 1))
        outs[1].start()
        y_copy(yp, 0, 3, left).wait_recv()
        outs.append(out_copy(yp, 2))
        outs[2].start()
        far = lax.rem(iy + 2, NY)
        y_copy(far, 0, 4, right).wait_recv()
        y_copy(far, 1, 5, left).wait_recv()
        outs.append(out_copy(far, 3))
        outs[3].start()
        for copy in sends + relay:
            copy.wait_send()

    for copy in xq + kv + returns:
        copy.wait_send()
    for h in range(2):
        for u in range(SUBS):
            for o in range(0, L):
                forward(h, u, o, o + 1, o, way[h][0]).wait_send()
            for o in range(NZ, L + 1, -1):
                forward(h, u, o % NZ, o - 1, o, way[h][1]).wait_send()
        for o in range(1, L + 1):
            for copy in send_state(h, o, o - 1, way[h][1]):
                copy.wait_send()
        for o in range(L + 1, NZ):
            for copy in send_state(h, o, o + 1, way[h][0]):
                copy.wait_send()
    for copy in outs:
        copy.wait()


def shards(NX, NZ, NY, queries, doc_of, doc_lengths, keys, values, key_scale, value_scale):
    rows, width = queries.shape
    cap = max(2, 3 * rows // (2 * NX))
    heads = width // HEAD_WIDTH
    _, span, cols = keys.shape
    half_n = NX * cap
    groups = 2 * half_n * GROUP // 128
    vmem, smem = pltpu.VMEM, pltpu.SMEM
    dma = pltpu.SemaphoreType.DMA
    signs = jnp.asarray(hadamard(), BF16)
    any_spec = pl.BlockSpec(memory_space=pl.ANY)
    return pl.pallas_call(
        functools.partial(kernel, NX, NZ, NY, cap),
        out_shape=jax.ShapeDtypeStruct((rows, width * NY), BF16),
        in_specs=[
            pl.BlockSpec(memory_space=vmem),
            pl.BlockSpec(memory_space=smem),
            pl.BlockSpec(memory_space=smem),
            pl.BlockSpec(memory_space=vmem),
            pl.BlockSpec(memory_space=vmem),
            pl.BlockSpec(memory_space=vmem),
            any_spec,
            any_spec,
        ],
        out_specs=any_spec,
        scratch_shapes=[
            vmem((rows * heads, HEAD_WIDTH), F32),
            vmem((rows, heads, HEAD_WIDTH), BF16),
            vmem((NX, 2, cap, GROUP, HEAD_WIDTH), BF16),
            vmem((NZ, 2 * half_n, GROUP, HEAD_WIDTH), BF16),
            vmem((2, span, HEAD_WIDTH), BF16),
            vmem((2, span, HEAD_WIDTH), BF16),
            vmem((2, 2, span), BF16),
            vmem((2, 2, span), BF16),
            vmem((2 * span, 2 * HEAD_WIDTH), BF16),
            vmem((HEAD_WIDTH + 16, 2 * span), BF16),
            vmem((2 * span, 256), F32),
            vmem((NZ, groups, 128, 128), F32),
            vmem((NZ, groups, 1, 128), F32),
            vmem((NZ, groups, 1, 128), F32),
            vmem((2, NZ, groups // 2, 128, 128), BF16),
            vmem((2, NZ, 8, 128), F32),
            vmem((2, NZ + 1, groups // 2, 128, 128), BF16),
            vmem((2, NZ + 1, 8, 128), F32),
            vmem((2 * half_n, GROUP, HEAD_WIDTH), BF16),
            vmem((NX * 2 * cap, GROUP, HEAD_WIDTH), BF16),
            vmem((NY, rows, width), BF16),
            dma((9,)),
            dma((4,)),
            dma((4,)),
            dma((NX, 2)),
            dma((NX, 2)),
            dma((2, SUBS, NZ + 1)),
            dma((2, SUBS, NZ + 1)),
            dma((2, NZ + 1)),
            dma((2, NZ + 1)),
            dma((2, NZ + 1)),
            dma((2, NZ + 1)),
            dma((NX, 2)),
            dma((NX, 2)),
            dma((6,)),
            dma((6,)),
        ],
        compiler_params=pltpu.CompilerParams(
            collective_id=0, has_side_effects=True, vmem_limit_bytes=60 * 1024 * 1024
        ),
    )(
        queries,
        doc_of,
        doc_lengths,
        signs,
        key_scale[0],
        value_scale[0],
        keys[0],
        values[0],
    )


def solution(mesh):
    in_specs = (
        P(("doc", "ctx"), "head"),
        P(("doc", "ctx"), None),
        P(),
        P("doc", "ctx", "head"),
        P("doc", "ctx", "head"),
        P("doc", "head", "ctx"),
        P("doc", "head", "ctx"),
    )
    out_specs = P(("doc", "ctx"), None)
    sizes = (mesh.shape["doc"], mesh.shape["ctx"] // 2, mesh.shape["head"])
    return jax.shard_map(
        functools.partial(shards, *sizes),
        mesh=mesh,
        in_specs=in_specs,
        out_specs=out_specs,
        check_vma=False,
    )
```

time: 272 us -> 78.3 us (0.29)
  the two profiles are of different devices: /device:TPU:128 before, /device:TPU:32 now
where the time goes in v1:
time: 78.3 us; the launch traced here: 78.2 us
  Pallas kernels  75 us (96%)
  local copies, waits for them, and re-layouts  3.2 us (4%)
    pallas_call x1, Pallas kernels, shards(): pl.pallas_call(functools.partial(kernel, NX, NZ, NY, cap), out_shape=jax....  75 us
    unnamed x4, local copies, waits for them, and re-layouts  3.2 us

profile of v1, /device:TPU:32, one launch (start us, length us, event | category | flops | bytes accessed | tf_op | source)
XLA Modules:
  0.0 78.2 jit_solution(951794285522867062)
XLA Ops:
  0.0 0.0 copy-start
  0.0 0.7 copy-done
  0.7 0.7 copy.9.doc_ref
  1.3 75.0 %shard_map.82 = bf16[16,16384]{1,0:T(8,128)(2,1)} custom-call(bf16[16,4096]{1,0:T(8,128)(2,1)} %q_ref.1, s32[16,1]{1,0:T(8,128)} %copy.9.doc_ref, s32[4]{0:T(128)} %len_ref.1, bf16[128,128]{1,0:T(8,128)(2,1)} %constant.2.clone.h_ref, bf16[2,1024]{1,0:T(2,128)(2,1)} %bitcast.6, bf16[2,1024]{1,0:T(2,128)(2,1)} %bitcast.7, bf16[1024,256]{1,0:T(8,128)(2,1)} %bitcast.4, ...), custom_call_target="tpu_custom_call" | custom-call | tf_op jit(solution)/shard_map/pallas_call | solution.py:503
  76.3 1.9 %copy.11 = bf16[16,16384]{1,0:T(8,128)(2,1)} copy(bf16[16,16384]{1,0:T(8,128)(2,1)} %shard_map.82) | data formatting | bytes 1048576
Async XLA Ops:
  0.0 0.7 copy-start
